TPU v7x, 32 devices: a whole 2x2x4 slice. The times are simulated.
32 devices in a mesh: rep: 2 (over y), ep: 8 (over z, core), tp: 2 (over x).
Axes of the slice: x: 2, y: 2, z: 4, core: 2. Of those that a mesh axis runs over, the one named last changes fastest.
Arguments:
- hidden_states: bfloat16 [2, 1024, 2048], P(None, ('rep', 'ep'), 'tp'), parts along dimension 1, may hold values from -8 to 8
- queries: bfloat16 [2, 1024, 4096], P(None, ('rep', 'ep'), 'tp'), parts along dimension 1, may hold values from -8 to 8
- fresh_key_value: bfloat16 [2, 1024, 2, 512], P(None, ('rep', 'ep'), None, 'tp'), parts along dimension 1, may hold values from -8 to 8
- cache: bfloat16 [16, 2, 1024, 512], P(('rep', 'ep'), None, None, 'tp'), parts along dimension 0, may hold values from -8 to 8
- cache_lengths: int32 [16], P(('rep', 'ep')), parts along dimension 0, may hold values from 1 to 1024, 4096 in all
- out_weight: bfloat16 [4096, 2048], P('tp', 'ep'), may hold values from -1 to 1
- router_weight: bfloat16 [2048, 16], P('tp'), may hold values from -0.125 to 0.125
- expert_weights: bfloat16 [16, 3, 2048, 384], P('ep', None, 'tp'), may hold values from -0.21875 to 0.21875
- expert_ids: int32 [2, 1024, 8], P(None, ('rep', 'ep')), parts along dimension 1, may hold values from 0 to 15, all different within a row; in each aligned block of 64 rows (0 to 63, 64 to 127, ..., all dimensions but the last counted through in order) at most 48 rows name the same one
- old_slots: int32 [16], replicated, may hold values from 0 to 15, as said below
- new_slots: int32 [16], replicated, may hold values from 0 to 15, as said below
- moved_experts: int32 [4], replicated, may hold values from 0 to 15, as said below
Outputs:
- mixed: bfloat16 [2, 1024, 2048], P(None, ('rep', 'ep'), 'tp'), parts along dimension 1
There are 2 independent parts, one for each index of `rep`. A program takes and returns all parts, laid end to end along the dimension named above; an argument that names none is the same for every part. Nothing has to cross between parts.
Inputs may be any that keep to these rules, and one draw needn't show every extreme that they name: `expert_ids`: each row names 8 different experts. Within the 64 rows of one request in one token block, no expert is named by more than 48 rows, a bound that some block reaches. `old_slots`: A permutation: each slot holds one expert. `new_slots`: equal to old_slots except at the moved experts, which take one another's old slots, none keeping its own. `moved_experts`: 4 different experts; no two of their old slots s share the same s // 2.
All inputs are finite; a program needn't handle non-finite values. No bound on the sum of `cache_lengths` on one device may be relied on, other than what follows from the above.
Results may differ from a plain program's by a relative error of at most 0.017.
Values may be sent and summed in bfloat16 or wider, within the bound.
A program may use at most 64 MiB of HBM per device.

v0:
```python
import jax
import jax.numpy as jnp
from jax import lax
from jax.sharding import PartitionSpec as P

D = 2048
HEAD_SIZE = 128


def lookup(entries, wanted_keys):
    return jnp.sum(
        jnp.where(
            wanted_keys[..., None] == jnp.arange(entries.shape[0], dtype=jnp.int32), entries, 0
        ),
        -1,
    )


def attend_local(queries, fresh_key_value, cache, cache_lengths):
    tokens_dev = queries.shape[1]
    kv_heads = fresh_key_value.shape[3] // HEAD_SIZE
    query_group_width = queries.shape[2] // HEAD_SIZE // kv_heads
    key_matrix = jnp.concatenate(
        [cache[0, 0], fresh_key_value[0, :, 0], fresh_key_value[1, :, 0]], 0
    )
    value_matrix = jnp.concatenate(
        [cache[0, 1], fresh_key_value[0, :, 1], fresh_key_value[1, :, 1]], 0
    )
    key_total = key_matrix.shape[0]
    context = cache.shape[2]
    query_matrix = queries.reshape(2 * tokens_dev, kv_heads, query_group_width, HEAD_SIZE)
    attention_scores = jnp.einsum(
        "meqt,wet->eqmw",
        query_matrix,
        key_matrix.reshape(key_total, kv_heads, HEAD_SIZE),
        preferred_element_type=jnp.float32,
    ) * HEAD_SIZE ** (-0.5)
    position = jnp.arange(key_total, dtype=jnp.int32)[None, :]
    row_index = jnp.arange(2 * tokens_dev, dtype=jnp.int32)[:, None]
    visible = jnp.where(
        position < context, position < cache_lengths[0], position - context <= row_index
    )
    attention_scores = jnp.where(visible, attention_scores, jnp.float32(-1e30))
    largest = jnp.max(attention_scores, -1, keepdims=True)
    weights = jnp.where(visible, jnp.exp(attention_scores - largest), jnp.float32(0.0))
    route_probability = (weights / jnp.sum(weights, -1, keepdims=True)).astype(jnp.bfloat16)
    layer_result = jnp.einsum(
        "qizo,oqx->zqix",
        route_probability,
        value_matrix.reshape(key_total, kv_heads, HEAD_SIZE),
        preferred_element_type=jnp.float32,
    )
    return layer_result.reshape(2 * tokens_dev, -1).astype(jnp.bfloat16)


def run_slots(weights, received):
    gate_up = jnp.einsum(
        "secq,egqf->secgf", received, weights[:, :2], preferred_element_type=jnp.float32
    )
    summed = lax.psum(gate_up.astype(jnp.bfloat16), "tp").astype(jnp.float32)
    hidden = (jax.nn.silu(summed[:, :, :, 0]) * summed[:, :, :, 1]).astype(jnp.bfloat16)
    layer_result = jnp.einsum(
        "secf,eqf->secq", hidden, weights[:, 2], preferred_element_type=jnp.float32
    ).astype(jnp.bfloat16)
    return lax.all_to_all(layer_result, "ep", split_axis=0, concat_axis=0, tiled=True)


def mix_block(normed_rows, resid_rows, routed, combine, slot_table, weights, capacity, groups):
    tokens_dev, top_count = routed.shape
    experts = slot_table.shape[0]
    local_slots = weights.shape[0]
    quarter = normed_rows.shape[1]
    slot_index = lookup(slot_table, routed)
    picked_mask = routed[:, :, None] == jnp.arange(experts, dtype=jnp.int32)[None, None, :]
    expert_marks = picked_mask.any(1).astype(jnp.bfloat16)
    earlier = (jnp.arange(tokens_dev)[:, None] > jnp.arange(tokens_dev)[None, :]).astype(
        jnp.bfloat16
    )
    before = jnp.dot(earlier, expert_marks, preferred_element_type=jnp.float32)
    slot_rank = jnp.sum(jnp.where(picked_mask, before[:, None, :], 0.0), -1).astype(jnp.int32)
    buffer_row = (slot_index * capacity + slot_rank).reshape(-1)
    buffer_rows = (
        jnp.zeros((groups * local_slots * capacity, quarter), jnp.bfloat16)
        .at[buffer_row]
        .set(jnp.repeat(normed_rows, top_count, axis=0))
    )
    outgoing = buffer_rows.reshape(groups, local_slots, capacity, quarter)
    returned = run_slots(
        weights, lax.all_to_all(outgoing, "ep", split_axis=0, concat_axis=0, tiled=True)
    )
    gathered = returned.reshape(-1, quarter)[buffer_row].reshape(tokens_dev, top_count, quarter)
    mixed_rows = resid_rows.astype(jnp.float32) + jnp.sum(
        combine[:, :, None] * gathered.astype(jnp.float32), 1
    )
    return mixed_rows.astype(jnp.bfloat16)


def relocate(expert_weights, old_slots, new_slots, moved_experts):
    local_slots = expert_weights.shape[0]
    groups = lax.axis_size("ep")
    flat_weights = expert_weights.reshape(local_slots, groups, -1)
    old_moved = lookup(old_slots, moved_experts)
    new_moved = lookup(new_slots, moved_experts)
    own_slots = lax.axis_index("ep") * local_slots + jnp.arange(local_slots, dtype=jnp.int32)
    leaving = (own_slots[:, None] == old_moved[None, :]).any(1)
    outgoing = jnp.sum(jnp.where(leaving[:, None, None], flat_weights, jnp.bfloat16(0.0)), 0)
    spread = lax.all_to_all(outgoing, "ep", split_axis=0, concat_axis=0, tiled=True)
    target_dev = new_moved // local_slots
    anchor_dev = old_moved // local_slots
    matches = jnp.arange(groups, dtype=jnp.int32)[:, None] == target_dev[None, :]
    anchor = jnp.sum(jnp.where(matches, anchor_dev[None, :], 0), 1)
    picked = jnp.where(matches.any(1)[:, None], spread[anchor], jnp.bfloat16(0.0))
    landed = lax.all_to_all(picked, "ep", split_axis=0, concat_axis=0, tiled=True)
    arriving = (own_slots[:, None] == new_moved[None, :]).any(1)
    return jnp.where(
        arriving[:, None, None, None],
        landed.reshape(expert_weights.shape[1:])[None],
        expert_weights,
    )


def per_device(
    hidden_states,
    queries,
    fresh_key_value,
    cache,
    cache_lengths,
    out_weight,
    router_weight,
    expert_weights,
    expert_ids,
    old_slots,
    new_slots,
    moved_experts,
):
    tokens_dev = hidden_states.shape[1]
    quarter = hidden_states.shape[2]
    experts = router_weight.shape[1]
    top_count = expert_ids.shape[2]
    groups = lax.axis_size("ep")
    capacity = min(tokens_dev, 3 * tokens_dev * top_count // (2 * experts))
    attention = attend_local(queries, fresh_key_value, cache, cache_lengths)
    head_terms = jnp.dot(
        attention,
        lax.all_gather(out_weight, "ep", axis=1, tiled=True),
        preferred_element_type=jnp.float32,
    )
    attn_out = lax.psum_scatter(
        head_terms.astype(jnp.bfloat16), "tp", scatter_dimension=1, tiled=True
    ).astype(jnp.float32)
    residual = (
        hidden_states.reshape(2 * tokens_dev, quarter).astype(jnp.float32) + attn_out
    ).astype(jnp.bfloat16)
    wide = residual.astype(jnp.float32)
    squares = lax.psum(jnp.sum(wide * wide, 1), "tp")
    normed = (wide * lax.rsqrt(squares / D + 1e-06)[:, None]).astype(jnp.bfloat16)
    logits = lax.psum(
        jnp.dot(normed, router_weight, preferred_element_type=jnp.float32).astype(jnp.bfloat16),
        "tp",
    ).astype(jnp.float32)
    routed = expert_ids.reshape(2 * tokens_dev, top_count)
    selected = jnp.sum(
        jnp.where(
            routed[:, :, None] == jnp.arange(experts, dtype=jnp.int32)[None, None, :],
            logits[:, None, :],
            0.0,
        ),
        -1,
    )
    raised = jnp.exp(selected)
    combine = raised / jnp.sum(raised, 1, keepdims=True)
    weights_two = relocate(expert_weights, old_slots, new_slots, moved_experts)
    outputs = []
    for block_index, slot_table, weights in (
        (0, old_slots, expert_weights),
        (1, new_slots, weights_two),
    ):
        lower = block_index * tokens_dev
        upper = lower + tokens_dev
        outputs.append(
            mix_block(
                normed[lower:upper],
                residual[lower:upper],
                routed[lower:upper],
                combine[lower:upper],
                slot_table,
                weights,
                capacity,
                groups,
            )
        )
    return jnp.stack(outputs)


def solution(mesh):
    return jax.shard_map(
        per_device,
        mesh=mesh,
        in_specs=(
            P(None, ("rep", "ep"), "tp"),
            P(None, ("rep", "ep"), "tp"),
            P(None, ("rep", "ep"), None, "tp"),
            P(("rep", "ep"), None, None, "tp"),
            P(("rep", "ep")),
            P("tp", "ep"),
            P("tp", None),
            P("ep", None, "tp", None),
            P(None, ("rep", "ep"), None),
            P(),
            P(),
            P(),
        ),
        out_specs=P(None, ("rep", "ep"), "tp"),
        check_vma=False,
    )
```

profile of v0, /device:TPU:0, one launch (start us, length us, event | category | flops | bytes accessed | tf_op | source)
XLA Modules:
  0.0 492.9 jit_solution(13353196676988205239)
XLA Ops:
  7.6 4.8 select_reduce_fusion
  17.0 15.5 %reduce.7 = bf16[8,147456]{1,0:T(8,128)(2,1)S(1)} reduce(bf16[8,1,147456]{2,1,0:T(2,128)(2,1)} %all_to_all.32, bf16[]{:T(256)} %broadcast.258), dimensions={1}, to_apply=%all_to_all.32.reduce_sub_computation | reduce | bytes 4718594 | tf_op jit(solution)/shard_map/all_to_all | solution.py:107
  36.0 6.4 %all-to-all-start.2 = ((bf16[8,2,73728]{2,1,0:T(2,128)(2,1)}), bf16[8,2,73728]{2,1,0:T(2,128)(2,1)S(1)}, u32[]{:S(2)}, u32[]{:S(2)}) async-start(bf16[8,2,73728]{2,1,0:T(2,128)(2,1)} %reshape.319), calls=%async_computation.3 | async-start | bytes 4718592 | tf_op jit(solution)/shard_map/all_to_all | solution.py:107
  53.9 9.2 %fusion.94 = (f32[2,8,128]{2,1,0:T(8,128)}, f32[2,8,128,1152]{2,3,1,0:T(8,128)}) fusion(pred[128,1152]{0,1:T(8,128)(4,1)} %fusion.61, bf16[128,2,8,128]{3,2,1,0:T(8,128)(2,1)S(1)} %bitcast.180, bf16[64,2,128]{2,0,1:T(8,128)(2,1)S(1)} %get-tuple-element.35, bf16[64,2,128]{2,0,1:T(8,128)(2,1)} %get-tuple-element.36, bf16[1024,2,128]{2,0,1:T(8,128)(2,1)} %copy.102), kind=kOutput, calls=%fused_computation.146 | convolution fusion | flops 617546880 | bytes 10706944 | tf_op jit(solution)/shard_map/sub | solution.py:45
  63.1 86.6 %all-to-all-done.2 = bf16[8,2,73728]{2,1,0:T(2,128)(2,1)S(1)} async-done(((bf16[8,2,73728]{2,1,0:T(2,128)(2,1)}), bf16[8,2,73728]{2,1,0:T(2,128)(2,1)S(1)}, u32[]{:S(2)}, u32[]{:S(2)}) %all-to-all-start.2) | async-done | bytes 2359328 | tf_op jit(solution)/shard_map/all_to_all | solution.py:107
  149.6 4.6 reshape.320
  154.2 5.4 %copy.171 = bf16[8,1,147456]{2,0,1:T(8,128)(2,1)S(1)} copy(bf16[8,1,147456]{2,1,0:T(2,128)(2,1)} %reshape.320) | data formatting | bytes 4718592
  170.7 5.2 %reshape.321 = bf16[8,2,73728]{2,1,0:T(2,128)(2,1)} reshape(bf16[8,147456]{1,0:T(8,128)(2,1)} %reduce.8) | data formatting | bytes 4718592
  175.9 6.2 %all-to-all-start.3 = ((bf16[8,2,73728]{2,1,0:T(2,128)(2,1)}), bf16[8,2,73728]{2,1,0:T(2,128)(2,1)S(1)}, u32[]{:S(2)}, u32[]{:S(2)}) async-start(bf16[8,2,73728]{2,1,0:T(2,128)(2,1)} %reshape.321), calls=%async_computation.4 | async-start | bytes 4718592 | tf_op jit(solution)/shard_map/all_to_all | solution.py:113
  189.7 5.5 %convolution_convert_fusion = bf16[128,2048]{1,0:T(8,128)(2,1)} fusion(bf16[128,2048]{0,1:T(8,128)(2,1)S(1)} %bitcast.178, bf16[2048,2048]{1,0:T(8,128)(2,1)} %all-gather.2.cloned.1.call-done), kind=kOutput, calls=%fused_computation.23 | convolution fusion | flops 1074003968 | bytes 9437184 | tf_op jit(solution)/shard_map/dot_general | solution.py:143
  195.9 15.5 %reduce-scatter.2.cloned.1.call-done = bf16[128,1024]{1,0:T(8,128)(2,1)} async-done(((bf16[128,2048]{1,0:T(8,128)(2,1)}), bf16[128,1024]{1,0:T(8,128)(2,1)}) %reduce-scatter.2.cloned.1.call-update) | async-done | bytes 262160 | tf_op jit(solution)/shard_map/reduce_scatter | solution.py:148
  212.6 4.9 %psum.28 = f32[128]{0:T(128)S(1)} all-reduce(f32[128]{0:T(128)S(1)} %get-tuple-element.13), channel_id=1, replica_groups=mesh['rep'=2,'ep'=8,'tp'=2] {'tp'}, use_global_device_ids=true, to_apply=%region_4.5 | all-reduce | flops 128 | bytes 1024 | tf_op jit(solution)/shard_map/psum | solution.py:155
  221.6 15.2 %all-to-all-done.3 = bf16[8,2,73728]{2,1,0:T(2,128)(2,1)S(1)} async-done(((bf16[8,2,73728]{2,1,0:T(2,128)(2,1)}), bf16[8,2,73728]{2,1,0:T(2,128)(2,1)S(1)}, u32[]{:S(2)}, u32[]{:S(2)}) %all-to-all-start.3) | async-done | bytes 2359328 | tf_op jit(solution)/shard_map/all_to_all | solution.py:113
  245.1 33.8 %all-to-all-done = bf16[8,2,48,1024]{3,2,1,0:T(8,128)(2,1)} async-done(((bf16[8,2,48,1024]{3,2,1,0:T(8,128)(2,1)}), bf16[8,2,48,1024]{3,2,1,0:T(8,128)(2,1)}, u32[]{:S(2)}, u32[]{:S(2)}) %all-to-all-start) | async-done | bytes 1572896 | tf_op jit(solution)/shard_map/all_to_all | solution.py:89
  283.4 4.6 reshape.322
  288.0 14.8 %reduce.4 = bf16[8,147456]{1,0:T(8,128)(2,1)S(1)} reduce(bf16[8,1,147456]{2,1,0:T(2,128)(2,1)} %reshape.322, bf16[]{:T(256)} %constant.67), dimensions={1}, to_apply=%all_to_all.29.reduce_sub_computation | reduce | bytes 4718594 | tf_op jit(solution)/shard_map/all_to_all | solution.py:113
  305.4 6.0 %broadcast_select_fusion = bf16[2,3,1024,384]{3,2,1,0:T(8,128)(2,1)} fusion(bf16[2,3,1024,384]{3,2,1,0:T(8,128)(2,1)} %param.19, pred[2]{0:T(512)(128)(4,1)S(1)} %get-tuple-element.8, bf16[3,1024,384]{2,1,0:T(8,128)(2,1)} %broadcast_in_dim.207), kind=kLoop, calls=%fused_computation.14 | loop fusion | flops 2359296 | bytes 11796482 | tf_op jit(solution)/shard_map/jit(_where)/select_n | solution.py:115
  315.2 5.8 %all-to-all-done.4 = bf16[8,2,48,1024]{3,2,1,0:T(8,128)(2,1)} async-done(((bf16[8,2,48,1024]{3,2,1,0:T(8,128)(2,1)}), bf16[8,2,48,1024]{3,2,1,0:T(8,128)(2,1)}, u32[]{:S(2)}, u32[]{:S(2)}) %all-to-all-start.4) | async-done | bytes 1572896 | tf_op jit(solution)/shard_map/all_to_all | solution.py:89
  321.0 4.8 fusion.38
  325.8 67.7 %all-reduce.3.cloned.1.call-done = (bf16[8,2,48,2,384]{4,2,0,1,3:T(8,128)(2,1)}, bf16[8,2,48,2,384]{4,2,3,0,1:T(8,128)(2,1)}) async-done(((bf16[8,2,48,2,384]{4,2,0,1,3:T(8,128)(2,1)}, bf16[8,2,48,2,384]{4,2,3,0,1:T(8,128)(2,1)}), (bf16[8,2,48,2,384]{4,2,0,1,3:T(8,128)(2,1)}, bf16[8,2,48,2,384]{4,2,3,0,1:T(8,128)(2,1)})) %all-reduce.3.cloned.1.call-update) | async-done | bytes 2359312 | tf_op jit(solution)/shard_map/psum | solution.py:60
  398.7 4.7 all-to-all-start.5
  407.5 33.7 %all-to-all-done.5 = bf16[8,2,48,1024]{3,2,1,0:T(8,128)(2,1)S(1)} async-done(((bf16[8,2,48,1024]{3,2,1,0:T(8,128)(2,1)}), bf16[8,2,48,1024]{3,2,1,0:T(8,128)(2,1)S(1)}, u32[]{:S(2)}, u32[]{:S(2)}) %all-to-all-start.5) | async-done | bytes 1572896 | tf_op jit(solution)/shard_map/all_to_all | solution.py:65
  445.1 5.2 %psum.29 = bf16[128,16]{0,1:T(8,128)(2,1)S(1)} all-reduce(bf16[128,16]{0,1:T(8,128)(2,1)S(1)} %convolution_convert_fusion.3), channel_id=1, replica_groups=mesh['rep'=2,'ep'=8,'tp'=2] {'tp'}, use_global_device_ids=true, to_apply=%region_5.6 | all-reduce | flops 2048 | bytes 8192 | tf_op jit(solution)/shard_map/psum | solution.py:157
  455.3 27.2 %all-to-all-done.1 = bf16[8,2,48,1024]{3,2,1,0:T(8,128)(2,1)S(1)} async-done(((bf16[8,2,48,1024]{3,2,1,0:T(8,128)(2,1)}), bf16[8,2,48,1024]{3,2,1,0:T(8,128)(2,1)S(1)}, u32[]{:S(2)}, u32[]{:S(2)}) %all-to-all-start.1) | async-done | bytes 1572896 | tf_op jit(solution)/shard_map/all_to_all | solution.py:65
  (112 shorter events, 85.3 us)
Async XLA Ops:
  6.5 438.4 %copy-start = (bf16[1024,16]{0,1:T(8,128)(2,1)S(1)}, bf16[1024,16]{0,1:T(8,128)(2,1)}, u32[]{:S(2)}) copy-start(bf16[1024,16]{0,1:T(8,128)(2,1)} %param.18) | copy-start | bytes 98308
  36.0 113.7 %all-to-all-start.2 = ((bf16[8,2,73728]{2,1,0:T(2,128)(2,1)}), bf16[8,2,73728]{2,1,0:T(2,128)(2,1)S(1)}, u32[]{:S(2)}, u32[]{:S(2)}) async-start(bf16[8,2,73728]{2,1,0:T(2,128)(2,1)} %reshape.319), calls=%async_computation.3 | async-start | bytes 4718592 | tf_op jit(solution)/shard_map/all_to_all | solution.py:107
  42.3 147.4 %all-gather.2.cloned.1.call-start = ((), (), s32[]{:S(2)}) async-start(), calls=%async_computation.7 | async-start | bytes 9437184 | tf_op jit(solution)/shard_map/all_gather | solution.py:145
  175.9 6.4 %copy-start.6 = (s32[2,64,8]{1,2,0:T(8,128)S(1)}, s32[2,64,8]{1,2,0:T(8,128)}, u32[]{:S(2)}) copy-start(s32[2,64,8]{1,2,0:T(8,128)} %param.20) | copy-start | bytes 12292
  175.9 6.5 %copy-start.4 = (bf16[1,64,1,256]{3,2,1,0:T(2,128)(2,1)S(1)}, bf16[1,64,1,256]{3,2,1,0:T(2,128)(2,1)}, u32[]{:S(2)}) copy-start(bf16[1,64,1,256]{3,2,1,0:T(2,128)(2,1)} %get-tuple-element.24) | copy-start | bytes 98308
  175.9 60.9 %all-to-all-start.3 = ((bf16[8,2,73728]{2,1,0:T(2,128)(2,1)}), bf16[8,2,73728]{2,1,0:T(2,128)(2,1)S(1)}, u32[]{:S(2)}, u32[]{:S(2)}) async-start(bf16[8,2,73728]{2,1,0:T(2,128)(2,1)} %reshape.321), calls=%async_computation.4 | async-start | bytes 4718592 | tf_op jit(solution)/shard_map/all_to_all | solution.py:113
  182.1 3.0 copy-start.9
  182.1 29.3 %reduce-scatter.2.cloned.1.call-start = ((), (), s32[]{:S(2)}) async-start(), calls=%async_computation.8 | async-start | bytes 786432 | tf_op jit(solution)/shard_map/reduce_scatter | solution.py:148
  189.7 5.9 %copy-start.7 = (s32[16]{0:T(128)S(1)}, s32[16]{0:T(128)}, u32[]{:S(2)}) copy-start(s32[16]{0:T(128)} %param.22) | copy-start | bytes 196
  189.7 5.9 %copy-start.8 = (s32[16]{0:T(128)S(1)}, s32[16]{0:T(128)}, u32[]{:S(2)}) copy-start(s32[16]{0:T(128)} %param.21) | copy-start | bytes 196
  189.7 21.7 %copy-start.5 = (bf16[2,64,1024]{2,1,0:T(8,128)(2,1)S(1)}, bf16[2,64,1024]{2,1,0:T(8,128)(2,1)}, u32[]{:S(2)}) copy-start(bf16[2,64,1024]{2,1,0:T(8,128)(2,1)} %param.12) | copy-start | bytes 786436
  212.6 24.2 %copy-start.1 = (bf16[128,1024]{1,0:T(8,128)(2,1)}, bf16[128,1024]{1,0:T(8,128)(2,1)S(1)}, u32[]{:S(2)}) copy-start(bf16[128,1024]{1,0:T(8,128)(2,1)S(1)} %get-tuple-element.14) | copy-start | bytes 786436
  236.7 42.1 %all-to-all-start = ((bf16[8,2,48,1024]{3,2,1,0:T(8,128)(2,1)}), bf16[8,2,48,1024]{3,2,1,0:T(8,128)(2,1)}, u32[]{:S(2)}, u32[]{:S(2)}) async-start(bf16[8,2,48,1024]{3,2,1,0:T(8,128)(2,1)} %bitcast.175), calls=%async_computation.1 | async-start | bytes 3145728 | tf_op jit(solution)/shard_map/all_to_all | solution.py:89
  278.9 42.1 %all-to-all-start.4 = ((bf16[8,2,48,1024]{3,2,1,0:T(8,128)(2,1)}), bf16[8,2,48,1024]{3,2,1,0:T(8,128)(2,1)}, u32[]{:S(2)}, u32[]{:S(2)}) async-start(bf16[8,2,48,1024]{3,2,1,0:T(8,128)(2,1)} %bitcast.174), calls=%async_computation.5 | async-start | bytes 3145728 | tf_op jit(solution)/shard_map/all_to_all | solution.py:89
  283.2 110.3 %all-reduce.3.cloned.1.call-start = ((), (), s32[]{:S(2)}) async-start(), calls=%async_computation.9 | async-start | bytes 4718592 | tf_op jit(solution)/shard_map/psum | solution.py:60
  302.9 8.5 %slice-start = ((s8[4718592]{0:T(1024)(128)(4,1)}), s8[524288]{0:T(1024)(128)(4,1)S(1)}, s32[]{:S(2)}) async-start(s8[4718592]{0:T(1024)(128)(4,1)} %bitcast.171), calls=%async_computation.10 | async-start | bytes 1048576
  305.4 6.0 %slice-start.1 = ((s8[4718592]{0:T(1024)(128)(4,1)}), s8[4194304]{0:T(1024)(128)(4,1)S(1)}, s32[]{:S(2)}) async-start(s8[4718592]{0:T(1024)(128)(4,1)} %bitcast.171), calls=%async_computation.11 | async-start | bytes 8388608
  398.7 4.7 copy-start.3
  398.7 42.5 %all-to-all-start.5 = ((bf16[8,2,48,1024]{3,2,1,0:T(8,128)(2,1)}), bf16[8,2,48,1024]{3,2,1,0:T(8,128)(2,1)S(1)}, u32[]{:S(2)}, u32[]{:S(2)}) async-start(bf16[8,2,48,1024]{3,2,1,0:T(8,128)(2,1)} %copy.120), calls=%async_computation.6 | async-start | bytes 3145728 | tf_op jit(solution)/shard_map/all_to_all | solution.py:65
  441.2 41.3 %all-to-all-start.1 = ((bf16[8,2,48,1024]{3,2,1,0:T(8,128)(2,1)}), bf16[8,2,48,1024]{3,2,1,0:T(8,128)(2,1)S(1)}, u32[]{:S(2)}, u32[]{:S(2)}) async-start(bf16[8,2,48,1024]{3,2,1,0:T(8,128)(2,1)} %copy.113), calls=%async_computation.2 | async-start | bytes 3145728 | tf_op jit(solution)/shard_map/all_to_all | solution.py:65
  482.6 2.8 copy-start.2
Sparse Core Ops, SparseCore 0:
  44.7 121.8 all-gather.1
  195.4 16.0 reduce-scatter.1
  325.9 67.5 all-reduce.2
where the time goes:
time: 500 us; the launch traced here: 493 us
  waiting for transfers between devices  286 us (57%)
  local copies, waits for them, and re-layouts  61.7 us (12%)
  other arithmetic  57.2 us (11%)
  matrix products  33.2 us (7%)
  starting transfers between devices  30 us (6%)
  between operations  14.5 us (3%)
  blocking collectives  10.1 us (2%)
    all_to_all x1, waiting for transfers between devices, relocate(): lax.all_to_all(outgoing, 'ep', split_axis=0, concat_axis=0, tiled=True)  86.6 us
    psum x1, waiting for transfers between devices, run_slots(): summed = lax.psum(gate_up.astype(jnp.bfloat16), 'tp').astype(jnp.float32)  67.7 us
    all_to_all x2, waiting for transfers between devices, run_slots(): lax.all_to_all(layer_result, 'ep', split_axis=0, concat_axis=0, tiled=True)  61 us
    all_to_all x2, waiting for transfers between devices, mix_block(): lax.all_to_all(outgoing, 'ep', split_axis=0, concat_axis=0, tiled=True)  39.5 us
    unnamed x32, local copies, waits for them, and re-layouts  25.7 us
    reduce_scatter x1, waiting for transfers between devices, per_device(): lax.psum_scatter(head_terms.astype(jnp.bfloat16), 'tp', scatter_dimension...  15.5 us
    all_to_all x1, other arithmetic, relocate(): lax.all_to_all(outgoing, 'ep', split_axis=0, concat_axis=0, tiled=True)  15.5 us
    all_to_all x1, waiting for transfers between devices, relocate(): lax.all_to_all(picked, 'ep', split_axis=0, concat_axis=0, tiled=True)  15.2 us
  transfers between devices with their start and end apart: 9, of which 8 were waited for; matrix products, arithmetic and copies ran while one was open for 22% of the time, Pallas kernels for 0%

commit v1 on v0

--- a/solution.py
+++ b/solution.py
@@ -1,10 +1,20 @@
+import functools
 import jax
 import jax.numpy as jnp
 from jax import lax
 from jax.sharding import PartitionSpec as P
+from jax.lax import all_gather
 
 D = 2048
 HEAD_SIZE = 128
+
+
+def treat_yards(my_tile, device_axis):
+    response = jnp.sum(all_gather(my_tile, device_axis), axis=0)
+    return response
+
+
+weights_update = functools.partial(treat_yards, device_axis="tp")
 
 
 def lookup(entries, wanted_keys):
@@ -57,7 +67,7 @@
     gate_up = jnp.einsum(
         "secq,egqf->secgf", received, weights[:, :2], preferred_element_type=jnp.float32
     )
-    summed = lax.psum(gate_up.astype(jnp.bfloat16), "tp").astype(jnp.float32)
+    summed = weights_update(gate_up.astype(jnp.bfloat16)).astype(jnp.float32)
     hidden = (jax.nn.silu(summed[:, :, :, 0]) * summed[:, :, :, 1]).astype(jnp.bfloat16)
     layer_result = jnp.einsum(
         "secf,eqf->secq", hidden, weights[:, 2], preferred_element_type=jnp.float32

time: 500 us -> 437 us (0.87)
  waiting for transfers between devices: 286 us -> 221 us
    psum x1 -> x0, waiting for transfers between devices: 67.7 us -> none  [run_slots(): summed = lax.psum(gate_up.astype(jnp.bfloat16), 'tp').astype(jnp.float32)]
    all_gather x0 -> x2, waiting for transfers between devices: none -> 30.7 us  [treat_yards(): response = jnp.sum(all_gather(my_tile, device_axis), axis=0)]
    all_to_all x2, waiting for transfers between devices: 61 us -> 32.2 us  [run_slots(): lax.all_to_all(layer_result, 'ep', split_axis=0, concat_axis=0, tiled=True)]
    unnamed x32 -> x30, local copies, waits for them, and re-layouts: 25.7 us -> 27.8 us
  transfers between devices with their start and end apart: 9 -> 10, of which waited for: 8 -> 9; matrix products, arithmetic and copies ran while one was open for 22% -> 28% of each run, Pallas kernels for 0% -> 0%
where the time goes in v1:
time: 437 us; the launch traced here: 430 us
  waiting for transfers between devices  221 us (51%)
  local copies, waits for them, and re-layouts  63.9 us (15%)
  other arithmetic  57.4 us (13%)
  matrix products  33.3 us (8%)
  starting transfers between devices  29.7 us (7%)
  between operations  14.4 us (3%)
  blocking collectives  9.87 us (2%)
    all_to_all x1, waiting for transfers between devices, relocate(): lax.all_to_all(outgoing, 'ep', split_axis=0, concat_axis=0, tiled=True)  86.6 us
    all_to_all x2, waiting for transfers between devices, mix_block(): lax.all_to_all(outgoing, 'ep', split_axis=0, concat_axis=0, tiled=True)  40.3 us
    all_to_all x2, waiting for transfers between devices, run_slots(): lax.all_to_all(layer_result, 'ep', split_axis=0, concat_axis=0, tiled=True)  32.2 us
    all_gather x2, waiting for transfers between devices, treat_yards(): response = jnp.sum(all_gather(my_tile, device_axis), axis=0)  30.7 us
    unnamed x30, local copies, waits for them, and re-layouts  27.8 us
    reduce_scatter x1, waiting for transfers between devices, per_device(): lax.psum_scatter(head_terms.astype(jnp.bfloat16), 'tp', scatter_dimension...  15.5 us
    all_to_all x1, other arithmetic, relocate(): lax.all_to_all(outgoing, 'ep', split_axis=0, concat_axis=0, tiled=True)  15.5 us
    all_to_all x1, waiting for transfers between devices, relocate(): lax.all_to_all(picked, 'ep', split_axis=0, concat_axis=0, tiled=True)  15.2 us
  transfers between devices with their start and end apart: 10, of which 9 were waited for; matrix products, arithmetic and copies ran while one was open for 28% of the time, Pallas kernels for 0%

profile of v1, /device:TPU:0, one launch (start us, length us, event | category | flops | bytes accessed | tf_op | source)
XLA Modules:
  0.0 430.0 jit_solution(16037849742900792322)
XLA Ops:
  7.6 4.8 %select_reduce_fusion = bf16[3,1024,384]{2,1,0:T(8,128)(2,1)S(1)} fusion(bf16[2,3,1024,384]{3,2,1,0:T(8,128)(2,1)} %param.19, pred[2]{0:T(512)(128)(4,1)S(1)} %get-tuple-element.7), kind=kLoop, calls=%fused_computation.11 | loop fusion | flops 3538944 | bytes 7077890 | tf_op jit(solution)/shard_map/reduce_sum | solution.py:116
  17.0 15.5 %reduce.9 = bf16[8,147456]{1,0:T(8,128)(2,1)S(1)} reduce(bf16[8,1,147456]{2,1,0:T(2,128)(2,1)} %all_to_all.32, bf16[]{:T(256)} %broadcast.258), dimensions={1}, to_apply=%all_to_all.32.reduce_sub_computation | reduce | bytes 4718594 | tf_op jit(solution)/shard_map/all_to_all | solution.py:117
  36.0 6.4 %all-to-all-start.2 = ((bf16[8,2,73728]{2,1,0:T(2,128)(2,1)}), bf16[8,2,73728]{2,1,0:T(2,128)(2,1)S(1)}, u32[]{:S(2)}, u32[]{:S(2)}) async-start(bf16[8,2,73728]{2,1,0:T(2,128)(2,1)} %reshape.321), calls=%async_computation.3 | async-start | bytes 4718592 | tf_op jit(solution)/shard_map/all_to_all | solution.py:117
  53.8 9.2 %fusion.88 = (f32[2,8,128]{2,1,0:T(8,128)}, f32[2,8,128,1152]{2,3,1,0:T(8,128)}) fusion(pred[128,1152]{0,1:T(8,128)(4,1)} %fusion.55, bf16[128,2,8,128]{3,2,1,0:T(8,128)(2,1)S(1)} %bitcast.184, bf16[64,2,128]{2,0,1:T(8,128)(2,1)S(1)} %get-tuple-element.33, bf16[64,2,128]{2,0,1:T(8,128)(2,1)} %get-tuple-element.34, bf16[1024,2,128]{2,0,1:T(8,128)(2,1)} %copy.98), kind=kOutput, calls=%fused_computation.145 | convolution fusion | flops 617546880 | bytes 10706944 | tf_op jit(solution)/shard_map/sub | solution.py:55
  63.0 86.6 %all-to-all-done.2 = bf16[8,2,73728]{2,1,0:T(2,128)(2,1)S(1)} async-done(((bf16[8,2,73728]{2,1,0:T(2,128)(2,1)}), bf16[8,2,73728]{2,1,0:T(2,128)(2,1)S(1)}, u32[]{:S(2)}, u32[]{:S(2)}) %all-to-all-start.2) | async-done | bytes 2359328 | tf_op jit(solution)/shard_map/all_to_all | solution.py:117
  149.6 4.6 %reshape.322 = bf16[8,1,147456]{2,1,0:T(2,128)(2,1)} reshape(bf16[8,2,73728]{2,1,0:T(2,128)(2,1)S(1)} %all-to-all-done.2) | data formatting | bytes 4718592
  154.2 5.4 %copy.162 = bf16[8,1,147456]{2,0,1:T(8,128)(2,1)S(1)} copy(bf16[8,1,147456]{2,1,0:T(2,128)(2,1)} %reshape.322) | data formatting | bytes 4718592
  170.7 5.2 %reshape.323 = bf16[8,2,73728]{2,1,0:T(2,128)(2,1)} reshape(bf16[8,147456]{1,0:T(8,128)(2,1)} %reduce.10) | data formatting | bytes 4718592
  175.9 6.2 %all-to-all-start.3 = ((bf16[8,2,73728]{2,1,0:T(2,128)(2,1)}), bf16[8,2,73728]{2,1,0:T(2,128)(2,1)S(1)}, u32[]{:S(2)}, u32[]{:S(2)}) async-start(bf16[8,2,73728]{2,1,0:T(2,128)(2,1)} %reshape.323), calls=%async_computation.4 | async-start | bytes 4718592 | tf_op jit(solution)/shard_map/all_to_all | solution.py:123
  185.1 4.6 %fusion.39 = bf16[2,128,8,128]{3,1,2,0:T(8,128)(2,1)S(1)} fusion(f32[2,8,128,1152]{2,3,1,0:T(8,128)} %get-tuple-element.30, f32[2,8,128]{2,1,0:T(8,128)S(1)} %copy-done.10, bf16[1152,2,128]{0,2,1:T(8,128)(2,1)S(1)} %concatenate.23), kind=kOutput, calls=%fused_computation.44 | convolution fusion | flops 608960512 | bytes 10559488 | tf_op jit(solution)/shard_map/qizo,oqx->zqix/dot_general | solution.py:57
  189.7 5.5 %convolution_convert_fusion = bf16[128,2048]{1,0:T(8,128)(2,1)} fusion(bf16[128,2048]{0,1:T(8,128)(2,1)S(1)} %bitcast.182, bf16[2048,2048]{1,0:T(8,128)(2,1)} %all-gather.6.cloned.1.call-done), kind=kOutput, calls=%fused_computation.22 | convolution fusion | flops 1074003968 | bytes 9437184 | tf_op jit(solution)/shard_map/dot_general | solution.py:153
  195.9 15.5 %reduce-scatter.2.cloned.1.call-done = bf16[128,1024]{1,0:T(8,128)(2,1)} async-done(((bf16[128,2048]{1,0:T(8,128)(2,1)}), bf16[128,1024]{1,0:T(8,128)(2,1)}) %reduce-scatter.2.cloned.1.call-update) | async-done | bytes 262160 | tf_op jit(solution)/shard_map/reduce_scatter | solution.py:158
  212.6 4.9 %psum.14 = f32[128]{0:T(128)S(1)} all-reduce(f32[128]{0:T(128)S(1)} %get-tuple-element.11), channel_id=1, replica_groups=mesh['rep'=2,'ep'=8,'tp'=2] {'tp'}, use_global_device_ids=true, to_apply=%region_4.5 | all-reduce | flops 128 | bytes 1024 | tf_op jit(solution)/shard_map/psum | solution.py:165
  221.5 15.2 %all-to-all-done.3 = bf16[8,2,73728]{2,1,0:T(2,128)(2,1)S(1)} async-done(((bf16[8,2,73728]{2,1,0:T(2,128)(2,1)}), bf16[8,2,73728]{2,1,0:T(2,128)(2,1)S(1)}, u32[]{:S(2)}, u32[]{:S(2)}) %all-to-all-start.3) | async-done | bytes 2359328 | tf_op jit(solution)/shard_map/all_to_all | solution.py:123
  241.2 4.6 %reshape.324 = bf16[8,1,147456]{2,1,0:T(2,128)(2,1)} reshape(bf16[8,2,73728]{2,1,0:T(2,128)(2,1)S(1)} %all-to-all-done.3) | data formatting | bytes 4718592
  245.8 14.8 %reduce.6 = bf16[8,147456]{1,0:T(8,128)(2,1)S(1)} reduce(bf16[8,1,147456]{2,1,0:T(2,128)(2,1)} %reshape.324, bf16[]{:T(256)} %constant.69), dimensions={1}, to_apply=%all_to_all.29.reduce_sub_computation | reduce | bytes 4718594 | tf_op jit(solution)/shard_map/all_to_all | solution.py:123
  267.2 11.7 %all-to-all-done.4 = bf16[8,2,48,1024]{3,2,1,0:T(8,128)(2,1)} async-done(((bf16[8,2,48,1024]{3,2,1,0:T(8,128)(2,1)}), bf16[8,2,48,1024]{3,2,1,0:T(8,128)(2,1)}, u32[]{:S(2)}, u32[]{:S(2)}) %all-to-all-start.4) | async-done | bytes 1572896 | tf_op jit(solution)/shard_map/all_to_all | solution.py:99
  292.3 28.7 %all-to-all-done = bf16[8,2,48,1024]{3,2,1,0:T(8,128)(2,1)} async-done(((bf16[8,2,48,1024]{3,2,1,0:T(8,128)(2,1)}), bf16[8,2,48,1024]{3,2,1,0:T(8,128)(2,1)}, u32[]{:S(2)}, u32[]{:S(2)}) %all-to-all-start) | async-done | bytes 1572896 | tf_op jit(solution)/shard_map/all_to_all | solution.py:99
  321.0 4.8 %fusion.32 = bf16[8,2,48,2,384]{4,2,3,0,1:T(8,128)(2,1)} fusion(bf16[2,3,1024,384]{3,2,1,0:T(8,128)(2,1)} %param.19, bf16[8,2,48,1024]{3,2,1,0:T(8,128)(2,1)} %all-to-all-done), kind=kOutput, calls=%fused_computation.42 | convolution fusion | flops 1208549376 | bytes 5898240 | tf_op jit(solution)/shard_map/secq,egqf->secgf/dot_general | solution.py:67
  335.9 4.6 %all-to-all-start.5 = ((bf16[8,2,48,1024]{3,2,1,0:T(8,128)(2,1)}), bf16[8,2,48,1024]{3,2,1,0:T(8,128)(2,1)S(1)}, u32[]{:S(2)}, u32[]{:S(2)}) async-start(bf16[8,2,48,1024]{3,2,1,0:T(8,128)(2,1)} %copy.116), calls=%async_computation.6 | async-start | bytes 3145728 | tf_op jit(solution)/shard_map/all_to_all | solution.py:75
  340.5 26.7 %all-gather.8.cloned.1.call-done = bf16[16,2,48,2,384]{4,2,3,0,1:T(8,128)(2,1)} async-done(((bf16[8,2,48,2,384]{4,2,3,0,1:T(8,128)(2,1)}), bf16[16,2,48,2,384]{4,2,3,0,1:T(8,128)(2,1)}) %all-gather.8.cloned.1.call-update) | async-done | bytes 2359312 | tf_op jit(solution)/shard_map/all_gather | solution.py:13
  373.6 4.7 %all-to-all-done.5 = bf16[8,2,48,1024]{3,2,1,0:T(8,128)(2,1)S(1)} async-done(((bf16[8,2,48,1024]{3,2,1,0:T(8,128)(2,1)}), bf16[8,2,48,1024]{3,2,1,0:T(8,128)(2,1)S(1)}, u32[]{:S(2)}, u32[]{:S(2)}) %all-to-all-start.5) | async-done | bytes 1572896 | tf_op jit(solution)/shard_map/all_to_all | solution.py:75
  382.2 4.9 %psum.15 = bf16[128,16]{0,1:T(8,128)(2,1)S(1)} all-reduce(bf16[128,16]{0,1:T(8,128)(2,1)S(1)} %convolution_convert_fusion.3), channel_id=1, replica_groups=mesh['rep'=2,'ep'=8,'tp'=2] {'tp'}, use_global_device_ids=true, to_apply=%region_5.6 | all-reduce | flops 2048 | bytes 8192 | tf_op jit(solution)/shard_map/psum | solution.py:167
  392.1 27.5 %all-to-all-done.1 = bf16[8,2,48,1024]{3,2,1,0:T(8,128)(2,1)S(1)} async-done(((bf16[8,2,48,1024]{3,2,1,0:T(8,128)(2,1)}), bf16[8,2,48,1024]{3,2,1,0:T(8,128)(2,1)S(1)}, u32[]{:S(2)}, u32[]{:S(2)}) %all-to-all-start.1) | async-done | bytes 1572896 | tf_op jit(solution)/shard_map/all_to_all | solution.py:75
  (114 shorter events, 93.0 us)
Async XLA Ops:
  6.5 375.5 %copy-start = (bf16[1024,16]{0,1:T(8,128)(2,1)S(1)}, bf16[1024,16]{0,1:T(8,128)(2,1)}, u32[]{:S(2)}) copy-start(bf16[1024,16]{0,1:T(8,128)(2,1)} %param.18) | copy-start | bytes 98308
  36.0 113.7 %all-to-all-start.2 = ((bf16[8,2,73728]{2,1,0:T(2,128)(2,1)}), bf16[8,2,73728]{2,1,0:T(2,128)(2,1)S(1)}, u32[]{:S(2)}, u32[]{:S(2)}) async-start(bf16[8,2,73728]{2,1,0:T(2,128)(2,1)} %reshape.321), calls=%async_computation.3 | async-start | bytes 4718592 | tf_op jit(solution)/shard_map/all_to_all | solution.py:117
  42.3 147.4 %all-gather.6.cloned.1.call-start = ((), (), s32[]{:S(2)}) async-start(), calls=%async_computation.7 | async-start | bytes 9437184 | tf_op jit(solution)/shard_map/all_gather | solution.py:155
  175.9 6.4 %copy-start.7 = (s32[2,64,8]{1,2,0:T(8,128)S(1)}, s32[2,64,8]{1,2,0:T(8,128)}, u32[]{:S(2)}) copy-start(s32[2,64,8]{1,2,0:T(8,128)} %param.20) | copy-start | bytes 12292
  175.9 6.5 %copy-start.5 = (bf16[1,64,1,256]{3,2,1,0:T(2,128)(2,1)S(1)}, bf16[1,64,1,256]{3,2,1,0:T(2,128)(2,1)}, u32[]{:S(2)}) copy-start(bf16[1,64,1,256]{3,2,1,0:T(2,128)(2,1)} %get-tuple-element.22) | copy-start | bytes 98308
  175.9 60.9 %all-to-all-start.3 = ((bf16[8,2,73728]{2,1,0:T(2,128)(2,1)}), bf16[8,2,73728]{2,1,0:T(2,128)(2,1)S(1)}, u32[]{:S(2)}, u32[]{:S(2)}) async-start(bf16[8,2,73728]{2,1,0:T(2,128)(2,1)} %reshape.323), calls=%async_computation.4 | async-start | bytes 4718592 | tf_op jit(solution)/shard_map/all_to_all | solution.py:123
  182.1 3.0 copy-start.10
  182.1 29.3 %reduce-scatter.2.cloned.1.call-start = ((), (), s32[]{:S(2)}) async-start(), calls=%async_computation.8 | async-start | bytes 786432 | tf_op jit(solution)/shard_map/reduce_scatter | solution.py:158
  189.7 5.9 %copy-start.8 = (s32[16]{0:T(128)S(1)}, s32[16]{0:T(128)}, u32[]{:S(2)}) copy-start(s32[16]{0:T(128)} %param.21) | copy-start | bytes 196
  189.7 5.9 %copy-start.9 = (s32[16]{0:T(128)S(1)}, s32[16]{0:T(128)}, u32[]{:S(2)}) copy-start(s32[16]{0:T(128)} %param.22) | copy-start | bytes 196
  189.7 21.7 %copy-start.6 = (bf16[2,64,1024]{2,1,0:T(8,128)(2,1)S(1)}, bf16[2,64,1024]{2,1,0:T(8,128)(2,1)}, u32[]{:S(2)}) copy-start(bf16[2,64,1024]{2,1,0:T(8,128)(2,1)} %param.12) | copy-start | bytes 786436
  212.6 24.2 %copy-start.3 = (bf16[128,1024]{1,0:T(8,128)(2,1)}, bf16[128,1024]{1,0:T(8,128)(2,1)S(1)}, u32[]{:S(2)}) copy-start(bf16[128,1024]{1,0:T(8,128)(2,1)S(1)} %get-tuple-element.12) | copy-start | bytes 786436
  236.7 42.1 %all-to-all-start.4 = ((bf16[8,2,48,1024]{3,2,1,0:T(8,128)(2,1)}), bf16[8,2,48,1024]{3,2,1,0:T(8,128)(2,1)}, u32[]{:S(2)}, u32[]{:S(2)}) async-start(bf16[8,2,48,1024]{3,2,1,0:T(8,128)(2,1)} %bitcast.176), calls=%async_computation.5 | async-start | bytes 3145728 | tf_op jit(solution)/shard_map/all_to_all | solution.py:99
  263.2 20.0 %copy-start.1 = (bf16[3,1024,384]{2,1,0:T(8,128)(2,1)S(1)}, bf16[3,1024,384]{2,1,0:T(8,128)(2,1)}, u32[]{:S(2)}) copy-start(bf16[3,1024,384]{2,1,0:T(8,128)(2,1)} %broadcast_in_dim.207) | copy-start | bytes 7077892
  278.8 42.1 %all-to-all-start = ((bf16[8,2,48,1024]{3,2,1,0:T(8,128)(2,1)}), bf16[8,2,48,1024]{3,2,1,0:T(8,128)(2,1)}, u32[]{:S(2)}, u32[]{:S(2)}) async-start(bf16[8,2,48,1024]{3,2,1,0:T(8,128)(2,1)} %bitcast.177), calls=%async_computation.1 | async-start | bytes 3145728 | tf_op jit(solution)/shard_map/all_to_all | solution.py:99
  283.2 46.6 %all-gather.10.cloned.1.call-start = ((), (), s32[]{:S(2)}) async-start(), calls=%async_computation.10 | async-start | bytes 3538944 | tf_op jit(solution)/shard_map/all_gather | solution.py:13
  286.2 2.1 copy-start.2
  292.2 75.0 %all-gather.8.cloned.1.call-start = ((), (), s32[]{:S(2)}) async-start(), calls=%async_computation.9 | async-start | bytes 3538944 | tf_op jit(solution)/shard_map/all_gather | solution.py:13
  335.9 42.4 %all-to-all-start.5 = ((bf16[8,2,48,1024]{3,2,1,0:T(8,128)(2,1)}), bf16[8,2,48,1024]{3,2,1,0:T(8,128)(2,1)S(1)}, u32[]{:S(2)}, u32[]{:S(2)}) async-start(bf16[8,2,48,1024]{3,2,1,0:T(8,128)(2,1)} %copy.116), calls=%async_computation.6 | async-start | bytes 3145728 | tf_op jit(solution)/shard_map/all_to_all | solution.py:75
  378.3 41.3 %all-to-all-start.1 = ((bf16[8,2,48,1024]{3,2,1,0:T(8,128)(2,1)}), bf16[8,2,48,1024]{3,2,1,0:T(8,128)(2,1)S(1)}, u32[]{:S(2)}, u32[]{:S(2)}) async-start(bf16[8,2,48,1024]{3,2,1,0:T(8,128)(2,1)} %copy.109), calls=%async_computation.2 | async-start | bytes 3145728 | tf_op jit(solution)/shard_map/all_to_all | solution.py:75
  419.6 2.8 copy-start.4
Sparse Core Ops, SparseCore 0:
  44.7 121.8 all-gather.5
  195.4 16.0 reduce-scatter.1
  292.4 37.3 all-gather.9
  331.1 36.0 all-gather.7
